TPU v7x, 32 devices: a whole 2x2x4 slice. The times are simulated.
32 devices in a mesh: gx: 4 (over y, x), gy: 8 (over z, core).
Axes of the slice: x: 2, y: 2, z: 4, core: 2. Of those that a mesh axis runs over, the one named last changes fastest.
Arguments:
- adjoint_temp: float32 [128, 256, 256], P('gx', 'gy'), may hold values from -6 to 6
- adjoint_load: float32 [128, 256, 256], P('gx', 'gy'), may hold values from -6 to 6
- conductivity: float32 [3, 128, 256, 256], P(None, 'gx', 'gy'), may hold values from 0.25 to 4
- expansion: float32 [3, 128, 256, 256], P(None, 'gx', 'gy'), may hold values from 0.5 to 2
- ref_temp: float32 [128, 256, 256], P('gx', 'gy'), may hold values from -4 to 4
- wall_rows: float32 [8192, 128], P(('gx', 'gy')), may hold values from -6 to 6
- wall_dest: int32 [8192, 1], P(('gx', 'gy')), may hold values from 0 to 31; in each aligned block of 256 rows (0 to 255, 256 to 511, ...) at most 9 rows name the same one
- wall_line: int32 [8192], P(('gx', 'gy')), may hold values from 0 to 2047
- wall_count: int32 [32], P(('gx', 'gy')), may hold values from 192 to 256, as said below
- tile_owner: int32 [32, 32], P(('gx', 'gy')), may hold values from 0 to 31, each once within a row
Outputs:
- adjoint_field: float32 [128, 256, 256], P('gx', 'gy')
- block_load: float32 [32, 3, 32, 8192], P(('gx', 'gy'))
Inputs may be any that keep to these rules, and one draw needn't show every extreme that they name: Each row of tile_owner names every elasticity block once. `wall_dest`: bricks are numbered with the span index slowest. Among the 256 row slots of one device, no brick is named by more than 9 of them. `wall_count`: some device has all 256 slots live.
All inputs are finite; a program needn't handle non-finite values.
Results may differ from a plain program's by a relative error of at most 0.0003.
Values sent between devices are 32-bit elements; how exact they have to be, the bound alone decides.
No kernel may reach another device: no remote copies, remote signals or barrier semaphores. Data moves between devices by JAX's collectives and lax.ppermute only.
A program may use at most 128 MiB of HBM per device.

v0:
```python
from functools import reduce
import jax
import jax.numpy as jnp
from jax import lax
from jax.sharding import PartitionSpec as P

OMEGA = 0.8
CLASS_WEIGHTS = (1.0, 0.25, 0.125)


def padded_2(block, sides, width):
    for axis, dim in sides:
        count = lax.axis_size(axis)
        forward = [(i, i + 1) for i in range(count - 1)]
        backward = [(target, source) for source, target in forward]
        low = lax.ppermute(
            lax.slice_in_dim(block, block.shape[dim] - width, None, axis=dim), axis, forward
        )
        high = lax.ppermute(lax.slice_in_dim(block, 0, width, axis=dim), axis, backward)
        block = jnp.concatenate([low, block, high], axis=dim)
    return block


def sweep(field_pad, conduct_pad, source, inside):
    padded = jnp.pad(field_pad, ((0, 0), (0, 0), (1, 1)))
    conduct = jnp.pad(conduct_pad, ((0, 0), (0, 0), (0, 0), (1, 1)))
    size_x = padded.shape[0] - 2
    size_y = padded.shape[1] - 2
    size_z = padded.shape[2] - 2
    center = padded[1:-1, 1:-1, 1:-1]
    coupled = jnp.zeros(center.shape, jnp.float32)
    diagonal = jnp.zeros(center.shape, jnp.float32)
    blends = {}
    for shift_x in (-1, 0, 1):
        for shift_y in (-1, 0, 1):
            for shift_z in (-1, 0, 1):
                shifts = (shift_x, shift_y, shift_z)
                axes_set = tuple((a for a in range(3) if shifts[a] != 0))
                if len(axes_set) == 0:
                    continue
                if axes_set not in blends:
                    blends[axes_set] = reduce(
                        lambda left, right: left + right, [conduct[a] for a in axes_set]
                    ) / float(len(axes_set))
                blended = blends[axes_set]
                local_k = blended[1:-1, 1:-1, 1:-1]
                across = lax.slice(
                    blended,
                    (1 + shift_x, 1 + shift_y, 1 + shift_z),
                    (1 + shift_x + size_x, 1 + shift_y + size_y, 1 + shift_z + size_z),
                )
                neighbour = lax.slice(
                    padded,
                    (1 + shift_x, 1 + shift_y, 1 + shift_z),
                    (1 + shift_x + size_x, 1 + shift_y + size_y, 1 + shift_z + size_z),
                )
                coupling = 0.5 * CLASS_WEIGHTS[len(axes_set) - 1] * (local_k + across)
                coupled = coupled + coupling * (center - neighbour)
                diagonal = diagonal + coupling
    applied = center + coupled
    return (center + OMEGA * (source - applied) / (1.0 + diagonal)) * inside


def exchange_rim(stacked, width):
    return padded_2(stacked, (("gx", 1), ("gy", 2)), width)


def body(
    adjoint_temp,
    adjoint_load,
    conductivity,
    expansion,
    ref_temp,
    wall_rows,
    wall_dest,
    wall_line,
    wall_count,
    tile_owner,
):
    span_count = lax.axis_size("gx")
    column_count = lax.axis_size("gy")
    devices = span_count * column_count
    size_x, size_y, size_z = adjoint_temp.shape
    rows_dev, row_width = wall_rows.shape
    segments = size_x * size_y * size_z // row_width
    capacity = (rows_dev + devices - 1) // devices + 1
    position = jnp.arange(rows_dev, dtype=jnp.int32)
    live = position < wall_count[0]
    target_brick = wall_dest[:, 0]
    labels = jnp.arange(devices, dtype=jnp.int32)
    onehot = ((target_brick[:, None] == labels[None, :]) & live[:, None]).astype(jnp.int32)
    earlier = jnp.cumsum(onehot, axis=0) - onehot
    slot_index = jnp.sum(earlier * onehot, axis=1)
    target = jnp.where(live, target_brick * capacity + slot_index, devices * capacity)
    send_rows = (
        jnp.zeros((devices * capacity, row_width), jnp.float32)
        .at[target]
        .set(wall_rows, mode="drop")
    )
    send_lines = (
        jnp.full((devices * capacity,), segments, jnp.int32).at[target].set(wall_line, mode="drop")
    )
    got_rows, got_lines = (
        lax.all_to_all(
            send_rows.reshape(devices, capacity, row_width),
            ("gx", "gy"),
            split_axis=0,
            concat_axis=0,
            tiled=True,
        ),
        lax.all_to_all(
            send_lines.reshape(devices, capacity),
            ("gx", "gy"),
            split_axis=0,
            concat_axis=0,
            tiled=True,
        ),
    )
    source = (
        adjoint_load.reshape(segments, row_width)
        .at[got_lines.reshape(-1)]
        .add(got_rows.reshape(-1, row_width), mode="drop")
        .reshape(size_x, size_y, size_z)
    )
    stacked = jnp.concatenate([adjoint_temp[None], conductivity], axis=0)
    padded = exchange_rim(stacked, 1)
    first = sweep(padded[0], padded[1:], source, 1.0)
    first_pad = exchange_rim(first[None], 1)[0]
    adjoint_field = sweep(first_pad, padded[1:], source, 1.0)
    thermal_load = expansion * (adjoint_field - ref_temp)[None]
    tile_cells = size_x * size_y * size_z // devices
    tiles = thermal_load.reshape(3, devices, tile_cells)
    matches = (tile_owner[0][:, None] == labels[None, :]).astype(jnp.int32)
    inverse = jnp.sum(matches * labels[:, None], axis=0)
    outgoing = jnp.take(tiles, inverse, axis=1)
    received = lax.all_to_all(outgoing, ("gx", "gy"), split_axis=1, concat_axis=1, tiled=True)
    return (adjoint_field, received[None])


def solution(mesh):
    placed = (
        P("gx", "gy", None),
        P("gx", "gy", None),
        P(None, "gx", "gy", None),
        P(None, "gx", "gy", None),
        P("gx", "gy", None),
        P(("gx", "gy"), None),
        P(("gx", "gy"), None),
        P(("gx", "gy")),
        P(("gx", "gy")),
        P(("gx", "gy"), None),
    )
    return jax.shard_map(
        body,
        mesh=mesh,
        in_specs=placed,
        out_specs=(P("gx", "gy", None), P(("gx", "gy"), None, None, None)),
        check_vma=False,
    )
```

profile of v0, /device:TPU:0, one launch (start us, length us, event | category | flops | bytes accessed | tf_op | source)
XLA Modules:
  0.0 257.6 jit_solution(10952993467441159841)
XLA Ops:
  0.7 1.8 pad_maximum_fusion.5
  2.5 4.9 %collective-permute-start = (f32[4,1,32,256]{3,2,1,0:T(8,128)}, f32[4,1,32,256]{3,2,1,0:T(8,128)S(1)}, u32[]{:S(2)}, u32[]{:S(2)}) collective-permute-start(f32[4,1,32,256]{3,2,1,0:T(8,128)} %get-tuple-element.21), channel_id=1, source_target_pairs={{0,8},{8,16},{16,24},{1,9},{9,17},{17,25},{2,10},{10,18},{18,26},{... | collective-permute-start | bytes 393224 | tf_op jit(solution)/shard_map/ppermute | solution.py:16
  7.4 1.3 collective-permute-start.1
  10.3 1.6 scatter_custom_fusion
  12.6 7.1 %all-to-all-start = ((s32[32,1,9]{2,1,0:T(1,128)}), s32[32,1,9]{2,1,0:T(1,128)}, u32[]{:S(2)}, u32[]{:S(2)}) async-start(s32[32,1,9]{2,1,0:T(1,128)} %bitcast.8), calls=%async_computation | async-start | bytes 32768 | tf_op jit(solution)/shard_map/all_to_all | solution.py:111
  19.8 2.0 pad_maximum_fusion.3
  21.9 2.7 %collective-permute-start.2 = (f32[4,34,1,256]{3,2,1,0:T(1,128)}, f32[4,34,1,256]{3,2,1,0:T(1,128)}, u32[]{:S(2)}, u32[]{:S(2)}) collective-permute-start(f32[4,34,1,256]{3,2,1,0:T(1,128)} %get-tuple-element.19), channel_id=1, source_target_pairs={{0,1},{1,2},{2,3},{3,4},{4,5},{5,6},{6,7},{8,9},{9,10},{10,11},{11... | collective-permute-start | bytes 417800 | tf_op jit(solution)/shard_map/ppermute | solution.py:16
  26.4 1.5 scatter_custom_fusion.1
  28.6 2.3 reshape.107
  30.9 7.5 %all-to-all-start.1 = ((f32[32,9,128]{2,1,0:T(8,128)}), f32[32,9,128]{2,1,0:T(8,128)}, u32[]{:S(2)}, u32[]{:S(2)}) async-start(f32[32,9,128]{2,1,0:T(8,128)} %reshape.110), calls=%async_computation.1 | async-start | bytes 524288 | tf_op jit(solution)/shard_map/all_to_all | solution.py:104
  38.9 1.4 reduce.7
  40.5 6.6 %select_maximum_fusion = f32[3,34,34,258]{3,2,1,0:T(8,128)S(1)} fusion(f32[4,34,1,256]{3,2,1,0:T(1,128)} %collective-permute-done.3, f32[4,34,1,256]{3,2,1,0:T(1,128)} %collective-permute-done.2, f32[4,1,32,256]{3,2,1,0:T(8,128)S(1)} %collective-permute-done.1, f32[4,1,32,256]{3,2,1,0:T(8,128)S(1)} %collective-permute-done, ...), kind=kLoop, calls=%fused_computation.6 | loop fusion | flops 12526416 | bytes 8313952 | tf_op jit(solution)/shard_map/concatenate | solution.py:20
  47.0 2.9 %add_multiply_fusion = (f32[34,34,258]{2,1,0:T(8,128)}, f32[34,34,258]{2,1,0:T(8,128)S(1)}, f32[34,34,258]{2,1,0:T(8,128)}, f32[34,34,258]{2,1,0:T(8,128)}) fusion(f32[3,34,34,258]{3,2,1,0:T(8,128)S(1)} %select_maximum_fusion), kind=kLoop, calls=%fused_computation.52 | loop fusion | flops 2385984 | bytes 8350944 | tf_op jit(solution)/shard_map/div | solution.py:42
  49.9 3.3 %slice_bitcast_fusion = (f32[34,34,258]{2,1,0:T(8,128)}, f32[34,34,258]{2,1,0:T(8,128)}, f32[34,34,258]{2,1,0:T(8,128)}) fusion(f32[3,34,34,258]{3,2,1,0:T(8,128)S(1)} %select_maximum_fusion), kind=kLoop, calls=%fused_computation.49 | loop fusion | bytes 7157952 | tf_op jit(solution)/shard_map/squeeze | solution.py:43
  55.4 1.6 reshape.142
  57.0 4.5 %scatter_fusion = f32[2048,128]{1,0:T(8,128)} fusion(f32[2048,128]{1,0:T(8,128)} %reshape.107, s32[288]{0:T(512)S(1)} %fusion.184, f32[288,128]{1,0:T(8,128)} %reshape.142), kind=kCustom, calls=%fused_computation.3 | custom fusion | flops 36864 | bytes 443520 | tf_op jit(solution)/shard_map/scatter-add | solution.py:122
  61.5 2.5 reshape.112
  64.0 24.5 %fusion.175 = f32[1,32,32,256]{3,2,1,0:T(8,128)S(1)} fusion(f32[32,32,256]{2,1,0:T(8,128)} %reshape.112, f32[34,34,256]{2,1,0:T(8,128)S(1)} %maximum_bitcast_fusion, f32[34,34,258]{2,1,0:T(8,128)S(1)} %get-tuple-element.16, f32[34,34,258]{2,1,0:T(8,128)} %get-tuple-element.18, f32[34,34,258]{2,1,0:T(8,128)} %get-tuple-element.17, ...), kind=kLoop, calls=%fused_computation.275 | loop fusion | flops 41943040 | bytes 47529984 | tf_op jit(solution)/shard_map/broadcast_in_dim | solution.py:128
  88.6 3.7 %collective-permute-start.4 = (f32[1,1,32,256]{3,2,1,0:T(8,128)S(1)}, f32[1,1,32,256]{3,2,1,0:T(8,128)S(1)}, u32[]{:S(2)}, u32[]{:S(2)}) collective-permute-start(f32[1,1,32,256]{3,2,1,0:T(8,128)S(1)} %get-tuple-element.25), channel_id=1, source_target_pairs={{0,8},{8,16},{16,24},{1,9},{9,17},{17,25},{2,10},{10,18},{18,26},{... | collective-permute-start | bytes 98312 | tf_op jit(solution)/shard_map/ppermute | solution.py:16
  92.3 1.3 collective-permute-start.5
  93.9 4.2 %collective-permute-done.5 = f32[1,1,32,256]{3,2,1,0:T(8,128)S(1)} collective-permute-done((f32[1,1,32,256]{3,2,1,0:T(8,128)S(1)}, f32[1,1,32,256]{3,2,1,0:T(8,128)S(1)}, u32[]{:S(2)}, u32[]{:S(2)}) %collective-permute-start.5) | collective-permute-done | bytes 32800 | tf_op jit(solution)/shard_map/ppermute | solution.py:19
  98.2 1.3 collective-permute-start.6
  100.8 3.5 %collective-permute-done.7 = f32[1,34,1,256]{3,2,1,0:T(1,128)S(1)} collective-permute-done((f32[1,34,1,256]{3,2,1,0:T(1,128)S(1)}, f32[1,34,1,256]{3,2,1,0:T(1,128)S(1)}, u32[]{:S(2)}, u32[]{:S(2)}) %collective-permute-start.7) | collective-permute-done | bytes 34848 | tf_op jit(solution)/shard_map/ppermute | solution.py:19
  104.3 1.4 maximum_bitcast_fusion.1
  105.7 25.7 %fusion.188 = (f32[32,32,256]{2,1,0:T(8,128)}, f32[32,32,256]{2,1,0:T(8,128)}) fusion(f32[32,32,256]{2,1,0:T(8,128)} %param.14, f32[32,32,256]{2,1,0:T(8,128)S(1)} %copy-done.4, f32[34,34,258]{2,1,0:T(8,128)S(1)} %get-tuple-element.16, f32[34,34,256]{2,1,0:T(8,128)S(1)} %maximum_bitcast_fusion.1, f32[34,34,258]{2,1,0:T(8,128)} %get-tuple-element.18, ...), kind=kLoop, calls=%fused_computation.314 | loop fusion | flops 42205184 | bytes 49627136 | tf_op jit(solution)/shard_map/sub | solution.py:130
  131.3 2.6 %broadcast_multiply_fusion = f32[3,32,32,256]{3,2,1,0:T(8,128)S(1)} fusion(f32[3,32,32,256]{3,2,1,0:T(8,128)} %param.13, f32[32,32,256]{2,1,0:T(8,128)} %get-tuple-element.10), kind=kLoop, calls=%fused_computation.55 | loop fusion | flops 786432 | bytes 7340032 | tf_op jit(solution)/shard_map/mul | solution.py:130
  133.9 2.3 reshape.113
  136.3 6.0 %copy.24 = f32[3,32,8192]{2,0,1:T(4,128)} copy(f32[3,32,8192]{2,1,0:T(8,128)} %reshape.113) | data formatting | bytes 6291456 | tf_op jit(solution)/shard_map/reshape | solution.py:132
  142.3 6.9 %gather_fusion = f32[32,3,8192]{2,1,0:T(4,128)} fusion(f32[3,32,8192]{2,0,1:T(4,128)} %copy.24, s32[1024]{0:T(1024)S(1)} %pad_clamp_fusion), kind=kCustom, calls=%fused_computation | custom fusion | bytes 6291584 | tf_op jit(solution)/shard_map/jit(_take)/gather | solution.py:135
  149.2 3.3 %select_bitcast_fusion = f32[3,32,8192]{2,0,1:T(4,128)S(1)} fusion(f32[32,3,8192]{2,1,0:T(4,128)} %gather_fusion, pred[32]{0:T(512)(128)(4,1)S(1)} %compare_and_fusion), kind=kLoop, calls=%fused_computation.48 | loop fusion | flops 786432 | bytes 6291488 | tf_op jit(solution)/shard_map/jit(_take)/select_n | solution.py:135
  152.6 101.6 %all_to_all.19 = f32[3,32,8192]{2,0,1:T(4,128)S(1)} all-to-all(f32[3,32,8192]{2,0,1:T(4,128)S(1)} %select_bitcast_fusion), channel_id=1, replica_groups=mesh['gx'=4,'gy'=8] {'gx','gy'}, dimensions={1} | all-to-all | bytes 6291456 | tf_op jit(solution)/shard_map/all_to_all | solution.py:136
  254.1 3.5 %copy.25 = f32[1,3,32,8192]{3,2,1,0:T(8,128)} copy(f32[1,3,32,8192]{3,1,2,0:T(4,128)S(1)} %bitcast.69) | data formatting | bytes 6291456
  (61 shorter events, 8.7 us)
Async XLA Ops:
  0.6 8.7 %copy-start.9 = (s32[256,1]{0,1:T(1,128)S(1)}, s32[256,1]{0,1:T(1,128)}, u32[]{:S(2)}) copy-start(s32[256,1]{0,1:T(1,128)} %param.16) | copy-start | bytes 3076
  0.6 19.1 %copy-start.12 = (s32[1,32]{1,0:T(1,128)S(1)}, s32[1,32]{1,0:T(1,128)}, u32[]{:S(2)}) copy-start(s32[1,32]{1,0:T(1,128)} %param.19) | copy-start | bytes 388
  0.6 19.2 %copy-start = (f32[3,32,32,256]{3,2,1,0:T(8,128)S(1)}, f32[3,32,32,256]{3,2,1,0:T(8,128)}, u32[]{:S(2)}) copy-start(f32[3,32,32,256]{3,2,1,0:T(8,128)} %param.12) | copy-start | bytes 9437188
  2.5 17.3 %collective-permute-start = (f32[4,1,32,256]{3,2,1,0:T(8,128)}, f32[4,1,32,256]{3,2,1,0:T(8,128)S(1)}, u32[]{:S(2)}, u32[]{:S(2)}) collective-permute-start(f32[4,1,32,256]{3,2,1,0:T(8,128)} %get-tuple-element.21), channel_id=1, source_target_pairs={{0,8},{8,16},{16,24},{1,9},{9,17},{17,25},{2,10},{10,18},{18,26},{... | collective-permute-start | bytes 393224 | tf_op jit(solution)/shard_map/ppermute | solution.py:16
  7.4 12.5 %collective-permute-start.1 = (f32[4,1,32,256]{3,2,1,0:T(8,128)}, f32[4,1,32,256]{3,2,1,0:T(8,128)S(1)}, u32[]{:S(2)}, u32[]{:S(2)}) collective-permute-start(f32[4,1,32,256]{3,2,1,0:T(8,128)} %get-tuple-element.22), channel_id=1, source_target_pairs={{8,0},{16,8},{24,16},{9,1},{17,9},{25,17},{10,2},{18,10},{26,18},{... | collective-permute-start | bytes 393224 | tf_op jit(solution)/shard_map/ppermute | solution.py:19
  10.3 11.6 %copy-start.10 = (s32[256,1]{0,1:T(1,128)}, s32[256,1]{0,1:T(1,128)S(1)}, u32[]{:S(2)}) copy-start(s32[256,1]{0,1:T(1,128)S(1)} %compare_select_fusion.1) | copy-start | bytes 3076
  12.6 18.4 %all-to-all-start = ((s32[32,1,9]{2,1,0:T(1,128)}), s32[32,1,9]{2,1,0:T(1,128)}, u32[]{:S(2)}, u32[]{:S(2)}) async-start(s32[32,1,9]{2,1,0:T(1,128)} %bitcast.8), calls=%async_computation | async-start | bytes 32768 | tf_op jit(solution)/shard_map/all_to_all | solution.py:111
  19.8 6.1 %copy-start.13 = (s32[32]{0:T(128)}, s32[32]{0:T(128)S(1)}, u32[]{:S(2)}) copy-start(s32[32]{0:T(128)S(1)} %select_reduce_fusion) | copy-start | bytes 388
  19.8 20.6 %copy-start.5 = (f32[4,1,32,256]{3,2,1,0:T(8,128)}, f32[4,1,32,256]{3,2,1,0:T(8,128)S(1)}, u32[]{:S(2)}) copy-start(f32[4,1,32,256]{3,2,1,0:T(8,128)S(1)} %collective-permute-done) | copy-start | bytes 393220
  19.8 20.6 %copy-start.7 = (f32[4,1,32,256]{3,2,1,0:T(8,128)}, f32[4,1,32,256]{3,2,1,0:T(8,128)S(1)}, u32[]{:S(2)}) copy-start(f32[4,1,32,256]{3,2,1,0:T(8,128)S(1)} %collective-permute-done.1) | copy-start | bytes 393220
  21.9 18.6 %collective-permute-start.2 = (f32[4,34,1,256]{3,2,1,0:T(1,128)}, f32[4,34,1,256]{3,2,1,0:T(1,128)}, u32[]{:S(2)}, u32[]{:S(2)}) collective-permute-start(f32[4,34,1,256]{3,2,1,0:T(1,128)} %get-tuple-element.19), channel_id=1, source_target_pairs={{0,1},{1,2},{2,3},{3,4},{4,5},{5,6},{6,7},{8,9},{9,10},{10,11},{11... | collective-permute-start | bytes 417800 | tf_op jit(solution)/shard_map/ppermute | solution.py:16
  24.6 15.9 %collective-permute-start.3 = (f32[4,34,1,256]{3,2,1,0:T(1,128)}, f32[4,34,1,256]{3,2,1,0:T(1,128)}, u32[]{:S(2)}, u32[]{:S(2)}) collective-permute-start(f32[4,34,1,256]{3,2,1,0:T(1,128)} %get-tuple-element.20), channel_id=1, source_target_pairs={{1,0},{2,1},{3,2},{4,3},{5,4},{6,5},{7,6},{9,8},{10,9},{11,10},{12... | collective-permute-start | bytes 417800 | tf_op jit(solution)/shard_map/ppermute | solution.py:19
  30.9 24.5 %all-to-all-start.1 = ((f32[32,9,128]{2,1,0:T(8,128)}), f32[32,9,128]{2,1,0:T(8,128)}, u32[]{:S(2)}, u32[]{:S(2)}) async-start(f32[32,9,128]{2,1,0:T(8,128)} %reshape.110), calls=%async_computation.1 | async-start | bytes 524288 | tf_op jit(solution)/shard_map/all_to_all | solution.py:104
  49.9 3.8 %copy-start.1 = (f32[3,32,32,256]{3,2,1,0:T(8,128)S(1)}, f32[3,32,32,256]{3,2,1,0:T(8,128)}, u32[]{:S(2)}) copy-start(f32[3,32,32,256]{3,2,1,0:T(8,128)} %param.12) | copy-start | bytes 9437188
  49.9 4.4 %copy-start.2 = (f32[32,32,256]{2,1,0:T(8,128)S(1)}, f32[32,32,256]{2,1,0:T(8,128)}, u32[]{:S(2)}) copy-start(f32[32,32,256]{2,1,0:T(8,128)} %param.10) | copy-start | bytes 3145732
  49.9 4.4 %copy-start.6 = (f32[4,1,32,256]{3,2,1,0:T(8,128)S(1)}, f32[4,1,32,256]{3,2,1,0:T(8,128)}, u32[]{:S(2)}) copy-start(f32[4,1,32,256]{3,2,1,0:T(8,128)} %copy-done.5) | copy-start | bytes 393220
  49.9 4.5 %copy-start.8 = (f32[4,1,32,256]{3,2,1,0:T(8,128)S(1)}, f32[4,1,32,256]{3,2,1,0:T(8,128)}, u32[]{:S(2)}) copy-start(f32[4,1,32,256]{3,2,1,0:T(8,128)} %copy-done.7) | copy-start | bytes 393220
  64.0 29.6 %copy-start.14 = (s32[32]{0:T(128)S(1)}, s32[32]{0:T(128)}, u32[]{:S(2)}) copy-start(s32[32]{0:T(128)} %copy-done.13) | copy-start | bytes 388
  64.0 36.8 %copy-start.11 = (s32[32]{0:T(128)S(1)}, s32[32]{0:T(128)}, u32[]{:S(2)}) copy-start(s32[32]{0:T(128)} %fusion.187) | copy-start | bytes 388
  88.5 12.3 %copy-start.3 = (f32[1,32,32,256]{3,2,1,0:T(8,128)}, f32[1,32,32,256]{3,2,1,0:T(8,128)S(1)}, u32[]{:S(2)}) copy-start(f32[1,32,32,256]{3,2,1,0:T(8,128)S(1)} %fusion.175) | copy-start | bytes 3145732
  88.5 17.1 %copy-start.4 = (f32[32,32,256]{2,1,0:T(8,128)S(1)}, f32[32,32,256]{2,1,0:T(8,128)}, u32[]{:S(2)}) copy-start(f32[32,32,256]{2,1,0:T(8,128)} %reshape.112) | copy-start | bytes 3145732
  88.6 5.3 %collective-permute-start.4 = (f32[1,1,32,256]{3,2,1,0:T(8,128)S(1)}, f32[1,1,32,256]{3,2,1,0:T(8,128)S(1)}, u32[]{:S(2)}, u32[]{:S(2)}) collective-permute-start(f32[1,1,32,256]{3,2,1,0:T(8,128)S(1)} %get-tuple-element.25), channel_id=1, source_target_pairs={{0,8},{8,16},{16,24},{1,9},{9,17},{17,25},{2,10},{10,18},{18,26},{... | collective-permute-start | bytes 98312 | tf_op jit(solution)/shard_map/ppermute | solution.py:16
  92.3 5.8 %collective-permute-start.5 = (f32[1,1,32,256]{3,2,1,0:T(8,128)S(1)}, f32[1,1,32,256]{3,2,1,0:T(8,128)S(1)}, u32[]{:S(2)}, u32[]{:S(2)}) collective-permute-start(f32[1,1,32,256]{3,2,1,0:T(8,128)S(1)} %get-tuple-element.26), channel_id=1, source_target_pairs={{8,0},{16,8},{24,16},{9,1},{17,9},{25,17},{10,2},{18,10},{26,18},{... | collective-permute-start | bytes 98312 | tf_op jit(solution)/shard_map/ppermute | solution.py:19
  98.2 2.6 %collective-permute-start.6 = (f32[1,34,1,256]{3,2,1,0:T(1,128)S(1)}, f32[1,34,1,256]{3,2,1,0:T(1,128)S(1)}, u32[]{:S(2)}, u32[]{:S(2)}) collective-permute-start(f32[1,34,1,256]{3,2,1,0:T(1,128)S(1)} %get-tuple-element.23), channel_id=1, source_target_pairs={{0,1},{1,2},{2,3},{3,4},{4,5},{5,6},{6,7},{8,9},{9,10},{10,11},{11... | collective-permute-start | bytes 104456 | tf_op jit(solution)/shard_map/ppermute | solution.py:16
  99.5 4.8 %collective-permute-start.7 = (f32[1,34,1,256]{3,2,1,0:T(1,128)S(1)}, f32[1,34,1,256]{3,2,1,0:T(1,128)S(1)}, u32[]{:S(2)}, u32[]{:S(2)}) collective-permute-start(f32[1,34,1,256]{3,2,1,0:T(1,128)S(1)} %get-tuple-element.24), channel_id=1, source_target_pairs={{1,0},{2,1},{3,2},{4,3},{5,4},{6,5},{7,6},{9,8},{10,9},{11,10},{12... | collective-permute-start | bytes 104456 | tf_op jit(solution)/shard_map/ppermute | solution.py:19
where the time goes:
time: 259 us; the launch traced here: 258 us
  blocking collectives  102 us (39%)
  other arithmetic  79 us (31%)
  local copies, waits for them, and re-layouts  35 us (14%)
  starting transfers between devices  32.3 us (12%)
  waiting for transfers between devices  7.96 us (3%)
    all_to_all x1, blocking collectives, body(): lax.all_to_all(outgoing, ('gx', 'gy'), split_axis=1, concat_axis=1, tiled...  102 us
    sub x1, other arithmetic, body(): thermal_load = expansion * (adjoint_field - ref_temp)[None]  25.7 us
    broadcast_in_dim x1, other arithmetic, body(): first_pad = exchange_rim(first[None], 1)[0]  24.5 us
    ppermute x4, starting transfers between devices, padded_2(): lax.ppermute(lax.slice_in_dim(block, block.shape[dim] - width, None, axis...  12.6 us
    reshape x2, local copies, waits for them, and re-layouts, body(): tiles = thermal_load.reshape(3, devices, tile_cells)  8.33 us
    ppermute x4, waiting for transfers between devices, padded_2(): lax.ppermute(lax.slice_in_dim(block, 0, width, axis=dim), axis, backward)  7.7 us
    all_to_all x1, starting transfers between devices, body(): lax.all_to_all(send_rows.reshape(devices, capacity, row_width), ('gx', 'g...  7.45 us
    all_to_all x1, starting transfers between devices, body(): lax.all_to_all(send_lines.reshape(devices, capacity), ('gx', 'gy'), split...  7.13 us
  transfers between devices with their start and end apart: 10, of which 3 were waited for; matrix products, arithmetic and copies ran while one was open for 10% of the time, Pallas kernels for 0%

commit v1 on v0

--- a/solution.py
+++ b/solution.py
@@ -133,7 +133,12 @@
     matches = (tile_owner[0][:, None] == labels[None, :]).astype(jnp.int32)
     inverse = jnp.sum(matches * labels[:, None], axis=0)
     outgoing = jnp.take(tiles, inverse, axis=1)
-    received = lax.all_to_all(outgoing, ("gx", "gy"), split_axis=1, concat_axis=1, tiled=True)
+    received = jnp.concatenate(
+        lax.all_to_all(
+            jnp.stack(jnp.split(outgoing, lax.axis_size(("gx", "gy")), axis=1)), ("gx", "gy"), 0, 0
+        ),
+        axis=1,
+    )
     return (adjoint_field, received[None])
 
 

time: 259 us -> 241 us (0.931)
  blocking collectives: 102 us -> 79.1 us
  local copies, waits for them, and re-layouts: 35 us -> 39.7 us
    all_to_all x1, blocking collectives: 102 us -> 79.1 us  [body(): lax.all_to_all(jnp.stack(jnp.split(outgoing, lax.axis_size(('gx', 'gy')),...]
    all_to_all x0 -> x1, local copies, waits for them, and re-layouts: none -> 3.85 us  [body(): lax.all_to_all(jnp.stack(jnp.split(outgoing, lax.axis_size(('gx', 'gy')),...]
    another operation x1 -> x3, local copies, waits for them, and re-layouts: 0.01 us -> 3.31 us  [the longest x2 3.31 us: body(): jnp.stack(jnp.split(outgoing, lax.axis_size(('gx', 'gy')), axis=1))]
  transfers between devices with their start and end apart: 10 -> 10, of which waited for: 3 -> 3; matrix products, arithmetic and copies ran while one was open for 10% -> 11% of each run, Pallas kernels for 0% -> 0%
where the time goes in v1:
time: 241 us; the launch traced here: 240 us
  blocking collectives  79.1 us (33%)
  other arithmetic  78.9 us (33%)
  local copies, waits for them, and re-layouts  39.7 us (16%)
  starting transfers between devices  32.3 us (13%)
  waiting for transfers between devices  7.96 us (3%)
    all_to_all x1, blocking collectives, body(): lax.all_to_all(jnp.stack(jnp.split(outgoing, lax.axis_size(('gx', 'gy')),...  79.1 us
    sub x1, other arithmetic, body(): thermal_load = expansion * (adjoint_field - ref_temp)[None]  25.6 us
    broadcast_in_dim x1, other arithmetic, body(): first_pad = exchange_rim(first[None], 1)[0]  24.5 us
    ppermute x4, starting transfers between devices, padded_2(): lax.ppermute(lax.slice_in_dim(block, block.shape[dim] - width, None, axis...  12.6 us
    reshape x2, local copies, waits for them, and re-layouts, body(): tiles = thermal_load.reshape(3, devices, tile_cells)  8.33 us
    ppermute x4, waiting for transfers between devices, padded_2(): lax.ppermute(lax.slice_in_dim(block, 0, width, axis=dim), axis, backward)  7.7 us
    all_to_all x1, starting transfers between devices, body(): lax.all_to_all(send_rows.reshape(devices, capacity, row_width), ('gx', 'g...  7.45 us
    all_to_all x1, starting transfers between devices, body(): lax.all_to_all(send_lines.reshape(devices, capacity), ('gx', 'gy'), split...  7.13 us
  transfers between devices with their start and end apart: 10, of which 3 were waited for; matrix products, arithmetic and copies ran while one was open for 11% of the time, Pallas kernels for 0%

profile of v1, /device:TPU:0, one launch (start us, length us, event | category | flops | bytes accessed | tf_op | source)
XLA Modules:
  0.0 240.0 jit_solution(8486346202934957755)
XLA Ops:
  0.7 1.8 pad_maximum_fusion.5
  2.5 4.9 %collective-permute-start = (f32[4,1,32,256]{3,2,1,0:T(8,128)}, f32[4,1,32,256]{3,2,1,0:T(8,128)S(1)}, u32[]{:S(2)}, u32[]{:S(2)}) collective-permute-start(f32[4,1,32,256]{3,2,1,0:T(8,128)} %get-tuple-element.19), channel_id=1, source_target_pairs={{0,8},{8,16},{16,24},{1,9},{9,17},{17,25},{2,10},{10,18},{18,26},{... | collective-permute-start | bytes 393224 | tf_op jit(solution)/shard_map/ppermute | solution.py:16
  7.4 1.3 collective-permute-start.1
  10.3 1.6 scatter_custom_fusion
  12.6 7.1 %all-to-all-start = ((s32[32,1,9]{2,1,0:T(1,128)}), s32[32,1,9]{2,1,0:T(1,128)}, u32[]{:S(2)}, u32[]{:S(2)}) async-start(s32[32,1,9]{2,1,0:T(1,128)} %bitcast.8), calls=%async_computation | async-start | bytes 32768 | tf_op jit(solution)/shard_map/all_to_all | solution.py:111
  19.8 2.0 pad_maximum_fusion.3
  21.8 2.7 %collective-permute-start.2 = (f32[4,34,1,256]{3,2,1,0:T(1,128)}, f32[4,34,1,256]{3,2,1,0:T(1,128)}, u32[]{:S(2)}, u32[]{:S(2)}) collective-permute-start(f32[4,34,1,256]{3,2,1,0:T(1,128)} %get-tuple-element.17), channel_id=1, source_target_pairs={{0,1},{1,2},{2,3},{3,4},{4,5},{5,6},{6,7},{8,9},{9,10},{10,11},{11... | collective-permute-start | bytes 417800 | tf_op jit(solution)/shard_map/ppermute | solution.py:16
  26.4 1.5 scatter_custom_fusion.1
  28.7 2.3 reshape.110
  30.9 7.5 %all-to-all-start.1 = ((f32[32,9,128]{2,1,0:T(8,128)}), f32[32,9,128]{2,1,0:T(8,128)}, u32[]{:S(2)}, u32[]{:S(2)}) async-start(f32[32,9,128]{2,1,0:T(8,128)} %reshape.113), calls=%async_computation.1 | async-start | bytes 524288 | tf_op jit(solution)/shard_map/all_to_all | solution.py:104
  38.9 1.4 reduce.7
  40.5 6.6 %select_maximum_fusion = f32[3,34,34,258]{3,2,1,0:T(8,128)S(1)} fusion(f32[4,34,1,256]{3,2,1,0:T(1,128)} %collective-permute-done.3, f32[4,34,1,256]{3,2,1,0:T(1,128)} %collective-permute-done.2, f32[4,1,32,256]{3,2,1,0:T(8,128)S(1)} %collective-permute-done.1, f32[4,1,32,256]{3,2,1,0:T(8,128)S(1)} %collective-permute-done, ...), kind=kLoop, calls=%fused_computation.6 | loop fusion | flops 12526416 | bytes 8313952 | tf_op jit(solution)/shard_map/concatenate | solution.py:20
  47.0 2.9 %add_multiply_fusion = (f32[34,34,258]{2,1,0:T(8,128)}, f32[34,34,258]{2,1,0:T(8,128)S(1)}, f32[34,34,258]{2,1,0:T(8,128)}, f32[34,34,258]{2,1,0:T(8,128)}) fusion(f32[3,34,34,258]{3,2,1,0:T(8,128)S(1)} %select_maximum_fusion), kind=kLoop, calls=%fused_computation.53 | loop fusion | flops 2385984 | bytes 8350944 | tf_op jit(solution)/shard_map/div | solution.py:42
  49.9 3.3 %slice_bitcast_fusion = (f32[34,34,258]{2,1,0:T(8,128)}, f32[34,34,258]{2,1,0:T(8,128)}, f32[34,34,258]{2,1,0:T(8,128)}) fusion(f32[3,34,34,258]{3,2,1,0:T(8,128)S(1)} %select_maximum_fusion), kind=kLoop, calls=%fused_computation.50 | loop fusion | bytes 7157952 | tf_op jit(solution)/shard_map/squeeze | solution.py:43
  55.4 1.6 reshape.146
  57.0 4.5 %scatter_fusion = f32[2048,128]{1,0:T(8,128)} fusion(f32[2048,128]{1,0:T(8,128)} %reshape.110, s32[288]{0:T(512)S(1)} %fusion.216, f32[288,128]{1,0:T(8,128)} %reshape.146), kind=kCustom, calls=%fused_computation.3 | custom fusion | flops 36864 | bytes 443520 | tf_op jit(solution)/shard_map/scatter-add | solution.py:122
  61.5 2.5 %reshape.115 = f32[32,32,256]{2,1,0:T(8,128)} reshape(f32[2048,128]{1,0:T(8,128)} %scatter_fusion) | data formatting | bytes 2097152 | tf_op jit(solution)/shard_map/reshape | solution.py:123
  64.0 24.5 %fusion.175 = f32[1,32,32,256]{3,2,1,0:T(8,128)S(1)} fusion(f32[32,32,256]{2,1,0:T(8,128)} %reshape.115, f32[34,34,256]{2,1,0:T(8,128)S(1)} %maximum_bitcast_fusion, f32[34,34,258]{2,1,0:T(8,128)S(1)} %get-tuple-element.14, f32[34,34,258]{2,1,0:T(8,128)} %get-tuple-element.16, f32[34,34,258]{2,1,0:T(8,128)} %get-tuple-element.15, ...), kind=kLoop, calls=%fused_computation.276 | loop fusion | flops 41943040 | bytes 47529984 | tf_op jit(solution)/shard_map/broadcast_in_dim | solution.py:128
  88.6 3.7 %collective-permute-start.4 = (f32[1,1,32,256]{3,2,1,0:T(8,128)S(1)}, f32[1,1,32,256]{3,2,1,0:T(8,128)S(1)}, u32[]{:S(2)}, u32[]{:S(2)}) collective-permute-start(f32[1,1,32,256]{3,2,1,0:T(8,128)S(1)} %get-tuple-element.23), channel_id=1, source_target_pairs={{0,8},{8,16},{16,24},{1,9},{9,17},{17,25},{2,10},{10,18},{18,26},{... | collective-permute-start | bytes 98312 | tf_op jit(solution)/shard_map/ppermute | solution.py:16
  92.3 1.3 collective-permute-start.5
  93.9 4.2 %collective-permute-done.5 = f32[1,1,32,256]{3,2,1,0:T(8,128)S(1)} collective-permute-done((f32[1,1,32,256]{3,2,1,0:T(8,128)S(1)}, f32[1,1,32,256]{3,2,1,0:T(8,128)S(1)}, u32[]{:S(2)}, u32[]{:S(2)}) %collective-permute-start.5) | collective-permute-done | bytes 32800 | tf_op jit(solution)/shard_map/ppermute | solution.py:19
  100.8 3.5 %collective-permute-done.7 = f32[1,34,1,256]{3,2,1,0:T(1,128)S(1)} collective-permute-done((f32[1,34,1,256]{3,2,1,0:T(1,128)S(1)}, f32[1,34,1,256]{3,2,1,0:T(1,128)S(1)}, u32[]{:S(2)}, u32[]{:S(2)}) %collective-permute-start.7) | collective-permute-done | bytes 34848 | tf_op jit(solution)/shard_map/ppermute | solution.py:19
  104.3 1.4 maximum_bitcast_fusion.1
  105.7 25.6 %fusion.220 = (f32[32,32,256]{2,1,0:T(8,128)}, f32[32,32,256]{2,1,0:T(8,128)}) fusion(f32[32,32,256]{2,1,0:T(8,128)} %param.14, f32[32,32,256]{2,1,0:T(8,128)S(1)} %copy-done.4, f32[34,34,258]{2,1,0:T(8,128)S(1)} %get-tuple-element.14, f32[34,34,256]{2,1,0:T(8,128)S(1)} %maximum_bitcast_fusion.1, f32[34,34,258]{2,1,0:T(8,128)} %get-tuple-element.16, ...), kind=kLoop, calls=%fused_computation.379 | loop fusion | flops 42205184 | bytes 49627136 | tf_op jit(solution)/shard_map/sub | solution.py:130
  131.2 2.6 %broadcast_multiply_fusion = f32[3,32,32,256]{3,2,1,0:T(8,128)S(1)} fusion(f32[3,32,32,256]{3,2,1,0:T(8,128)} %param.13, f32[32,32,256]{2,1,0:T(8,128)} %get-tuple-element.8), kind=kLoop, calls=%fused_computation.56 | loop fusion | flops 786432 | bytes 7340032 | tf_op jit(solution)/shard_map/mul | solution.py:130
  133.8 2.3 reshape.116
  136.2 6.0 %copy.61 = f32[3,32,8192]{2,0,1:T(4,128)} copy(f32[3,32,8192]{2,1,0:T(8,128)} %reshape.116) | data formatting | bytes 6291456 | tf_op jit(solution)/shard_map/reshape | solution.py:132
  142.2 6.9 %gather_fusion = f32[32,3,8192]{2,1,0:T(4,128)} fusion(f32[3,32,8192]{2,0,1:T(4,128)} %copy.61, s32[1024]{0:T(1024)S(1)} %pad_clamp_fusion), kind=kCustom, calls=%fused_computation | custom fusion | bytes 6291584 | tf_op jit(solution)/shard_map/jit(_take)/gather | solution.py:135
  149.1 3.3 %select_bitcast_fusion = f32[3,32,8192]{2,0,1:T(4,128)S(1)} fusion(f32[32,3,8192]{2,1,0:T(4,128)} %gather_fusion, pred[32]{0:T(512)(128)(4,1)S(1)} %compare_and_fusion), kind=kLoop, calls=%fused_computation.48 | loop fusion | flops 786432 | bytes 6291488 | tf_op jit(solution)/shard_map/jit(_take)/select_n | solution.py:135
  153.8 3.3 %copy.62 = f32[32,3,1,8192]{3,2,1,0:T(1,128)S(1)} copy(f32[32,3,1,8192]{3,1,2,0:T(4,128)S(1)} %fusion.176) | data formatting | bytes 6291456 | tf_op jit(solution)/shard_map/stack | solution.py:138
  157.0 79.1 %all_to_all.19 = f32[32,3,1,8192]{3,2,1,0:T(1,128)S(1)} all-to-all(f32[32,3,1,8192]{3,2,1,0:T(1,128)S(1)} %copy.62), channel_id=1, replica_groups=mesh['gx'=4,'gy'=8] {'gx','gy'}, dimensions={0} | all-to-all | bytes 6291456 | tf_op jit(solution)/shard_map/all_to_all | solution.py:137
  236.1 3.8 %copy.67 = f32[32,3,1,8192]{3,0,1,2:T(8,128)} copy(f32[32,3,1,8192]{3,2,1,0:T(1,128)S(1)} %all_to_all.19) | data formatting | bytes 6291456 | tf_op jit(solution)/shard_map/all_to_all | solution.py:137
  (94 shorter events, 11.0 us)
Async XLA Ops:
  0.6 19.2 %copy-start = (f32[3,32,32,256]{3,2,1,0:T(8,128)S(1)}, f32[3,32,32,256]{3,2,1,0:T(8,128)}, u32[]{:S(2)}) copy-start(f32[3,32,32,256]{3,2,1,0:T(8,128)} %param.12) | copy-start | bytes 9437188
  0.6 8.7 %copy-start.9 = (s32[256,1]{0,1:T(1,128)S(1)}, s32[256,1]{0,1:T(1,128)}, u32[]{:S(2)}) copy-start(s32[256,1]{0,1:T(1,128)} %param.16) | copy-start | bytes 3076
  0.7 19.0 %copy-start.12 = (s32[1,32]{1,0:T(1,128)S(1)}, s32[1,32]{1,0:T(1,128)}, u32[]{:S(2)}) copy-start(s32[1,32]{1,0:T(1,128)} %param.19) | copy-start | bytes 388
  2.5 17.3 %collective-permute-start = (f32[4,1,32,256]{3,2,1,0:T(8,128)}, f32[4,1,32,256]{3,2,1,0:T(8,128)S(1)}, u32[]{:S(2)}, u32[]{:S(2)}) collective-permute-start(f32[4,1,32,256]{3,2,1,0:T(8,128)} %get-tuple-element.19), channel_id=1, source_target_pairs={{0,8},{8,16},{16,24},{1,9},{9,17},{17,25},{2,10},{10,18},{18,26},{... | collective-permute-start | bytes 393224 | tf_op jit(solution)/shard_map/ppermute | solution.py:16
  7.4 12.5 %collective-permute-start.1 = (f32[4,1,32,256]{3,2,1,0:T(8,128)}, f32[4,1,32,256]{3,2,1,0:T(8,128)S(1)}, u32[]{:S(2)}, u32[]{:S(2)}) collective-permute-start(f32[4,1,32,256]{3,2,1,0:T(8,128)} %get-tuple-element.20), channel_id=1, source_target_pairs={{8,0},{16,8},{24,16},{9,1},{17,9},{25,17},{10,2},{18,10},{26,18},{... | collective-permute-start | bytes 393224 | tf_op jit(solution)/shard_map/ppermute | solution.py:19
  10.3 15.6 %copy-start.10 = (s32[256,1]{0,1:T(1,128)}, s32[256,1]{0,1:T(1,128)S(1)}, u32[]{:S(2)}) copy-start(s32[256,1]{0,1:T(1,128)S(1)} %compare_select_fusion.1) | copy-start | bytes 3076
  12.6 18.4 %all-to-all-start = ((s32[32,1,9]{2,1,0:T(1,128)}), s32[32,1,9]{2,1,0:T(1,128)}, u32[]{:S(2)}, u32[]{:S(2)}) async-start(s32[32,1,9]{2,1,0:T(1,128)} %bitcast.8), calls=%async_computation | async-start | bytes 32768 | tf_op jit(solution)/shard_map/all_to_all | solution.py:111
  19.8 6.1 %copy-start.13 = (s32[32]{0:T(128)}, s32[32]{0:T(128)S(1)}, u32[]{:S(2)}) copy-start(s32[32]{0:T(128)S(1)} %select_reduce_fusion) | copy-start | bytes 388
  19.8 27.2 %copy-start.5 = (f32[4,1,32,256]{3,2,1,0:T(8,128)}, f32[4,1,32,256]{3,2,1,0:T(8,128)S(1)}, u32[]{:S(2)}) copy-start(f32[4,1,32,256]{3,2,1,0:T(8,128)S(1)} %collective-permute-done) | copy-start | bytes 393220
  19.8 27.2 %copy-start.7 = (f32[4,1,32,256]{3,2,1,0:T(8,128)}, f32[4,1,32,256]{3,2,1,0:T(8,128)S(1)}, u32[]{:S(2)}) copy-start(f32[4,1,32,256]{3,2,1,0:T(8,128)S(1)} %collective-permute-done.1) | copy-start | bytes 393220
  21.8 18.6 %collective-permute-start.2 = (f32[4,34,1,256]{3,2,1,0:T(1,128)}, f32[4,34,1,256]{3,2,1,0:T(1,128)}, u32[]{:S(2)}, u32[]{:S(2)}) collective-permute-start(f32[4,34,1,256]{3,2,1,0:T(1,128)} %get-tuple-element.17), channel_id=1, source_target_pairs={{0,1},{1,2},{2,3},{3,4},{4,5},{5,6},{6,7},{8,9},{9,10},{10,11},{11... | collective-permute-start | bytes 417800 | tf_op jit(solution)/shard_map/ppermute | solution.py:16
  24.6 15.9 %collective-permute-start.3 = (f32[4,34,1,256]{3,2,1,0:T(1,128)}, f32[4,34,1,256]{3,2,1,0:T(1,128)}, u32[]{:S(2)}, u32[]{:S(2)}) collective-permute-start(f32[4,34,1,256]{3,2,1,0:T(1,128)} %get-tuple-element.18), channel_id=1, source_target_pairs={{1,0},{2,1},{3,2},{4,3},{5,4},{6,5},{7,6},{9,8},{10,9},{11,10},{12... | collective-permute-start | bytes 417800 | tf_op jit(solution)/shard_map/ppermute | solution.py:19
  30.9 24.5 %all-to-all-start.1 = ((f32[32,9,128]{2,1,0:T(8,128)}), f32[32,9,128]{2,1,0:T(8,128)}, u32[]{:S(2)}, u32[]{:S(2)}) async-start(f32[32,9,128]{2,1,0:T(8,128)} %reshape.113), calls=%async_computation.1 | async-start | bytes 524288 | tf_op jit(solution)/shard_map/all_to_all | solution.py:104
  49.9 3.8 %copy-start.1 = (f32[3,32,32,256]{3,2,1,0:T(8,128)S(1)}, f32[3,32,32,256]{3,2,1,0:T(8,128)}, u32[]{:S(2)}) copy-start(f32[3,32,32,256]{3,2,1,0:T(8,128)} %param.12) | copy-start | bytes 9437188
  49.9 4.4 %copy-start.2 = (f32[32,32,256]{2,1,0:T(8,128)S(1)}, f32[32,32,256]{2,1,0:T(8,128)}, u32[]{:S(2)}) copy-start(f32[32,32,256]{2,1,0:T(8,128)} %param.10) | copy-start | bytes 3145732
  49.9 4.4 %copy-start.6 = (f32[4,1,32,256]{3,2,1,0:T(8,128)S(1)}, f32[4,1,32,256]{3,2,1,0:T(8,128)}, u32[]{:S(2)}) copy-start(f32[4,1,32,256]{3,2,1,0:T(8,128)} %copy-done.5) | copy-start | bytes 393220
  49.9 4.5 %copy-start.8 = (f32[4,1,32,256]{3,2,1,0:T(8,128)S(1)}, f32[4,1,32,256]{3,2,1,0:T(8,128)}, u32[]{:S(2)}) copy-start(f32[4,1,32,256]{3,2,1,0:T(8,128)} %copy-done.7) | copy-start | bytes 393220
  64.0 29.6 %copy-start.14 = (s32[32]{0:T(128)S(1)}, s32[32]{0:T(128)}, u32[]{:S(2)}) copy-start(s32[32]{0:T(128)} %copy-done.13) | copy-start | bytes 388
  64.0 36.8 %copy-start.11 = (s32[32]{0:T(128)S(1)}, s32[32]{0:T(128)}, u32[]{:S(2)}) copy-start(s32[32]{0:T(128)} %fusion.219) | copy-start | bytes 388
  88.5 12.3 %copy-start.3 = (f32[1,32,32,256]{3,2,1,0:T(8,128)}, f32[1,32,32,256]{3,2,1,0:T(8,128)S(1)}, u32[]{:S(2)}) copy-start(f32[1,32,32,256]{3,2,1,0:T(8,128)S(1)} %fusion.175) | copy-start | bytes 3145732
  88.5 17.1 %copy-start.4 = (f32[32,32,256]{2,1,0:T(8,128)S(1)}, f32[32,32,256]{2,1,0:T(8,128)}, u32[]{:S(2)}) copy-start(f32[32,32,256]{2,1,0:T(8,128)} %reshape.115) | copy-start | bytes 3145732
  88.6 5.3 %collective-permute-start.4 = (f32[1,1,32,256]{3,2,1,0:T(8,128)S(1)}, f32[1,1,32,256]{3,2,1,0:T(8,128)S(1)}, u32[]{:S(2)}, u32[]{:S(2)}) collective-permute-start(f32[1,1,32,256]{3,2,1,0:T(8,128)S(1)} %get-tuple-element.23), channel_id=1, source_target_pairs={{0,8},{8,16},{16,24},{1,9},{9,17},{17,25},{2,10},{10,18},{18,26},{... | collective-permute-start | bytes 98312 | tf_op jit(solution)/shard_map/ppermute | solution.py:16
  92.3 5.8 %collective-permute-start.5 = (f32[1,1,32,256]{3,2,1,0:T(8,128)S(1)}, f32[1,1,32,256]{3,2,1,0:T(8,128)S(1)}, u32[]{:S(2)}, u32[]{:S(2)}) collective-permute-start(f32[1,1,32,256]{3,2,1,0:T(8,128)S(1)} %get-tuple-element.24), channel_id=1, source_target_pairs={{8,0},{16,8},{24,16},{9,1},{17,9},{25,17},{10,2},{18,10},{26,18},{... | collective-permute-start | bytes 98312 | tf_op jit(solution)/shard_map/ppermute | solution.py:19
  98.2 2.6 %collective-permute-start.6 = (f32[1,34,1,256]{3,2,1,0:T(1,128)S(1)}, f32[1,34,1,256]{3,2,1,0:T(1,128)S(1)}, u32[]{:S(2)}, u32[]{:S(2)}) collective-permute-start(f32[1,34,1,256]{3,2,1,0:T(1,128)S(1)} %get-tuple-element.21), channel_id=1, source_target_pairs={{0,1},{1,2},{2,3},{3,4},{4,5},{5,6},{6,7},{8,9},{9,10},{10,11},{11... | collective-permute-start | bytes 104456 | tf_op jit(solution)/shard_map/ppermute | solution.py:16
  99.5 4.8 %collective-permute-start.7 = (f32[1,34,1,256]{3,2,1,0:T(1,128)S(1)}, f32[1,34,1,256]{3,2,1,0:T(1,128)S(1)}, u32[]{:S(2)}, u32[]{:S(2)}) collective-permute-start(f32[1,34,1,256]{3,2,1,0:T(1,128)S(1)} %get-tuple-element.22), channel_id=1, source_target_pairs={{1,0},{2,1},{3,2},{4,3},{5,4},{6,5},{7,6},{9,8},{10,9},{11,10},{12... | collective-permute-start | bytes 104456 | tf_op jit(solution)/shard_map/ppermute | solution.py:19
